TPU v7x, 128 devices: a whole 4x4x4 slice. The times are simulated.
128 devices in a mesh: dp: 16 (over y, x), expert: 8 (over z, core).
Axes of the slice: x: 4, y: 4, z: 4, core: 2. Of those that a mesh axis runs over, the one named last changes fastest.
Arguments:
- tokens: bfloat16 [4096, 4096], P('dp', 'expert'), may hold values from -100 to 100
- w_gate: bfloat16 [8, 4096, 14336], P('expert', None, 'dp'), may hold values from -0.09375 to 0.09375
- w_up: bfloat16 [8, 4096, 14336], P('expert', None, 'dp'), may hold values from -0.09375 to 0.09375
- w_down: bfloat16 [8, 14336, 4096], P('expert', 'dp'), may hold values from -0.046875 to 0.046875
- pick_block: int32 [8, 8], replicated, may hold values from 0 to 3
- pick_live: int32 [8, 8], replicated, may hold values from 0 to 1, as said below
- combine_weight: float32 [8, 8], replicated, may hold values from 0.25 to 1
Outputs:
- combined: bfloat16 [4096, 4096], P('dp', 'expert')
Inputs may be any that keep to these rules, and one draw needn't show every extreme that they name: `pick_live`: each expert takes at least one block, and some expert takes a block from every pair of dp rows.
All inputs are finite; a program needn't handle non-finite values.
Results may differ from a plain program's by a relative error of at most 0.02.
Values may be sent and summed in bfloat16 or wider, within the bound.
A program may use at most 128 MiB of HBM per device.

v0:
```python
import jax
import jax.numpy as jnp
from jax import lax
from jax.sharding import PartitionSpec as P

BLOCK = 128


def from_partner(value, axis, stride):
    return lax.ppermute(value, axis, [(i, i ^ 1 << stride) for i in range(lax.axis_size(axis))])


def rms_normalize(values, square_sums, model_width):
    values_f32 = values.astype(jnp.float32)
    inv_rms = lax.rsqrt(square_sums / model_width + 1e-05)
    return (values_f32 * inv_rms[:, None]).astype(jnp.bfloat16)


def on_device(tokens, w_gate, w_up, w_down, pick_block, pick_live, combine_weight):
    expert_count = lax.axis_size("expert")
    features_dev = tokens.shape[1]
    model_width = features_dev * expert_count
    blocks_here = tokens.shape[0] // BLOCK
    half_rows = BLOCK // 2
    row_index = lax.axis_index("dp")
    half_bit = row_index % 2
    pair_index = row_index // 2
    tokens_f32 = tokens.astype(jnp.float32)
    square_sums = lax.psum(jnp.sum(tokens_f32 * tokens_f32, axis=1), "expert")
    source = rms_normalize(tokens, square_sums, model_width)
    picked = lax.dynamic_index_in_dim(pick_block, pair_index, axis=1, keepdims=False)
    live_flags = lax.dynamic_index_in_dim(pick_live, pair_index, axis=1, keepdims=False)
    weights_here = lax.dynamic_index_in_dim(combine_weight, pair_index, axis=1, keepdims=False)
    owned_here = (live_flags == 1) & (picked // blocks_here == half_bit)
    local_block = picked % blocks_here
    blocks = source.reshape(blocks_here, BLOCK, features_dev)
    chosen = jnp.take(blocks, local_block, axis=0)
    chosen = jnp.where(owned_here[:, None, None], chosen, jnp.zeros((), jnp.bfloat16))
    arrived = lax.all_to_all(chosen, "expert", split_axis=0, concat_axis=2, tiled=True)[0]
    outgoing = lax.dynamic_slice_in_dim(arrived, (1 - half_bit) * half_rows, half_rows, 0)
    partner = from_partner(outgoing, "dp", 0)
    own_half = lax.dynamic_slice_in_dim(arrived, half_bit * half_rows, half_rows, 0)
    merged = own_half + partner
    gate_weights = w_gate[0]
    up_weights = w_up[0]
    down_weights = w_down[0]
    rows_piece = lax.all_gather(merged, "dp", axis=0, tiled=True)
    gate_proj = jnp.dot(rows_piece, gate_weights, preferred_element_type=jnp.float32)
    up_proj = jnp.dot(rows_piece, up_weights, preferred_element_type=jnp.float32)
    hidden = (jax.nn.silu(gate_proj) * up_proj).astype(jnp.bfloat16)
    partial_value = jnp.dot(hidden, down_weights, preferred_element_type=jnp.float32).astype(
        jnp.bfloat16
    )
    summed = lax.psum_scatter(
        lax.optimization_barrier(partial_value).astype(jnp.float32).astype(jnp.bfloat16),
        "dp",
        scatter_dimension=0,
        tiled=True,
    )
    spread = lax.all_to_all(summed[:, None, :], "expert", split_axis=2, concat_axis=1, tiled=True)
    other_half = from_partner(spread, "dp", 0)
    assembled = jnp.where(
        half_bit == 0,
        jnp.concatenate([spread, other_half], axis=0),
        jnp.concatenate([other_half, spread], axis=0),
    )
    slot_match = local_block[None, :] == jnp.arange(blocks_here, dtype=jnp.int32)[:, None]
    combine_coef = jnp.where(
        slot_match & owned_here[None, :], weights_here[None, :], jnp.zeros((), jnp.float32)
    )
    combined = jnp.einsum("le,red->lrd", combine_coef, assembled.astype(jnp.float32))
    return combined.astype(jnp.bfloat16).reshape(blocks_here * BLOCK, features_dev)


def solution(mesh):
    in_specs = (
        P("dp", "expert"),
        P("expert", None, "dp"),
        P("expert", None, "dp"),
        P("expert", "dp", None),
        P(),
        P(),
        P(),
    )
    out_specs = P("dp", "expert")
    return jax.shard_map(
        on_device, mesh=mesh, in_specs=in_specs, out_specs=out_specs, check_vma=False
    )
```

profile of v0, /device:TPU:0, one launch (start us, length us, event | category | flops | bytes accessed | tf_op | source)
XLA Modules:
  0.0 329.2 jit_solution(12364163355996505817)
XLA Ops:
  6.5 0.0 copy-start
  6.5 0.9 dynamic-slice_reduce_fusion.1
  7.5 1.1 fusion.12
  8.6 16.0 %psum.7 = f32[256]{0:T(256)S(1)} all-reduce(f32[256]{0:T(256)S(1)} %fusion.12), channel_id=1, replica_groups=mesh['dp'=16,'expert'=8] {'expert'}, use_global_device_ids=true, to_apply=%region_1.2 | all-reduce | flops 256 | bytes 2048 | tf_op jit(solution)/shard_map/psum | solution.py:29
  24.5 1.1 fusion.13
  25.6 0.9 fusion.15
  26.5 0.6 gather_fusion
  27.2 1.2 select_select_fusion
  28.4 3.6 %all-to-all-start = ((bf16[8,128,512]{2,1,0:T(8,128)(2,1)}), bf16[8,128,512]{2,1,0:T(8,128)(2,1)S(1)}, u32[]{:S(2)}, u32[]{:S(2)}) async-start(bf16[8,128,512]{2,1,0:T(8,128)(2,1)} %select_select_fusion), calls=%async_computation | async-start | bytes 2097152 | tf_op jit(solution)/shard_map/all_to_all | solution.py:39
  31.9 0.0 all-gather.2.cloned.1.call-start
  32.0 15.8 %all-to-all-done = bf16[8,128,512]{2,1,0:T(8,128)(2,1)S(1)} async-done(((bf16[8,128,512]{2,1,0:T(8,128)(2,1)}), bf16[8,128,512]{2,1,0:T(8,128)(2,1)S(1)}, u32[]{:S(2)}, u32[]{:S(2)}) %all-to-all-start) | async-done | bytes 1048608 | tf_op jit(solution)/shard_map/all_to_all | solution.py:39
  47.8 0.7 copy.27
  48.5 0.6 constant_dynamic-slice_fusion
  49.1 0.4 copy.29
  49.5 1.6 collective-permute-start
  51.0 0.4 copy.33
  51.4 11.6 %collective-permute-done = bf16[64,4096]{1,0:T(8,128)(2,1)S(1)} collective-permute-done((bf16[64,4096]{1,0:T(8,128)(2,1)S(1)}, bf16[64,4096]{1,0:T(8,128)(2,1)S(1)}, u32[]{:S(2)}, u32[]{:S(2)}) %collective-permute-start) | collective-permute-done | bytes 524320 | tf_op jit(solution)/shard_map/ppermute | solution.py:10
  63.0 1.0 add.73
  64.0 0.0 all-gather.2.cloned.1.call-update
  64.0 0.2 reduce-scatter.2.cloned.1.call-start
  64.2 70.0 %all-gather.2.cloned.1.call-done = bf16[1024,4096]{1,0:T(8,128)(2,1)} async-done(((bf16[64,4096]{1,0:T(8,128)(2,1)}), bf16[1024,4096]{1,0:T(8,128)(2,1)}) %all-gather.2.cloned.1.call-update) | async-done | bytes 8388624 | tf_op jit(solution)/shard_map/all_gather | solution.py:47
  134.3 0.0 copy-start.1
  134.3 12.5 %fusion.1 = f32[1024,896]{1,0:T(8,128)S(1)} fusion(bf16[1024,4096]{1,0:T(8,128)(2,1)} %all-gather.2.cloned.1.call-done, bf16[1,4096,896]{2,1,0:T(8,128)(2,1)} %param.9), kind=kOutput, calls=%fused_computation.3 | convolution fusion | flops 7516192768 | bytes 19398656 | tf_op jit(solution)/shard_map/dot_general | solution.py:49
  146.8 0.0 copy-done.1
  146.8 15.1 %fusion.3 = f32[1024,896]{1,0:T(8,128)S(1)} fusion(bf16[1024,4096]{1,0:T(8,128)(2,1)S(1)} %copy-done.1, bf16[1,4096,896]{2,1,0:T(8,128)(2,1)} %param.8), kind=kOutput, calls=%fused_computation.5 | convolution fusion | flops 7516192768 | bytes 19398656 | tf_op jit(solution)/shard_map/dot_general | solution.py:48
  161.9 14.1 %convolution_convert_fusion = bf16[1024,4096]{1,0:T(8,128)(2,1)} fusion(bf16[1,896,4096]{2,1,0:T(8,128)(2,1)} %param.10, f32[1024,896]{1,0:T(8,128)S(1)} %fusion.1, f32[1024,896]{1,0:T(8,128)S(1)} %fusion.3), kind=kOutput, calls=%fused_computation.1 | convolution fusion | flops 7525892096 | bytes 23068672 | tf_op jit(solution)/shard_map/dot_general | solution.py:51
  176.0 0.0 reduce-scatter.2.cloned.1.call-update
  176.0 84.8 %reduce-scatter.2.cloned.1.call-done = bf16[64,4096]{1,0:T(8,128)(2,1)} async-done(((bf16[1024,4096]{1,0:T(8,128)(2,1)}), bf16[64,4096]{1,0:T(8,128)(2,1)}) %reduce-scatter.2.cloned.1.call-update) | async-done | bytes 524304 | tf_op jit(solution)/shard_map/reduce_scatter | solution.py:54
  260.7 4.9 %copy.30 = bf16[64,1,4096]{0,1,2:T(2,128)(2,1)S(1)} copy(bf16[64,1,4096]{2,0,1:T(8,128)(2,1)} %bitcast.33) | data formatting | bytes 1048576 | tf_op jit(solution)/shard_map/broadcast_in_dim | solution.py:60
  265.6 0.5 broadcast.170
  266.1 22.6 %reduce.10 = bf16[4096,64]{1,0:T(8,128)(2,1)S(1)} reduce(bf16[4096,1,64]{2,1,0:T(2,128)(2,1)S(1)} %bitcast.29, bf16[]{:T(256)} %broadcast.170), dimensions={1}, to_apply=%bitcast.23.reduce_sub_computation | reduce | bytes 1048578
  288.8 0.7 reshape.126
  289.5 14.6 %all_to_all.27 = bf16[8,2,16384]{2,1,0:T(2,128)(2,1)S(1)} all-to-all(bf16[8,2,16384]{2,1,0:T(2,128)(2,1)S(1)} %reshape.126), channel_id=1, replica_groups=mesh['dp'=16,'expert'=8] {'expert'}, dimensions={0} | all-to-all | bytes 1048576 | tf_op jit(solution)/shard_map/all_to_all | solution.py:60
  304.1 1.2 reshape.127
  305.4 2.3 copy.31
  307.6 0.2 copy.34
  307.8 1.5 collective-permute-start.1
  309.3 0.0 copy-done
  309.3 0.2 dynamic-slice_reduce_fusion
  309.5 11.7 %collective-permute-done.1 = bf16[64,8,512]{2,1,0:T(8,128)(2,1)S(1)} collective-permute-done((bf16[64,8,512]{2,1,0:T(8,128)(2,1)S(1)}, bf16[64,8,512]{2,1,0:T(8,128)(2,1)S(1)}, u32[]{:S(2)}, u32[]{:S(2)}) %collective-permute-start.1) | collective-permute-done | bytes 524320 | tf_op jit(solution)/shard_map/ppermute | solution.py:10
  321.2 0.4 convolution_convert_fusion.1
  321.6 0.7 copy.32
  (4 shorter events, 0.0 us)
Async XLA Ops:
  6.5 302.8 %copy-start = (f32[8,8]{1,0:T(8,128)S(1)}, f32[8,8]{1,0:T(8,128)}, u32[]{:S(2)}) copy-start(f32[8,8]{1,0:T(8,128)} %param.13) | copy-start | bytes 772
  28.4 19.4 %all-to-all-start = ((bf16[8,128,512]{2,1,0:T(8,128)(2,1)}), bf16[8,128,512]{2,1,0:T(8,128)(2,1)S(1)}, u32[]{:S(2)}, u32[]{:S(2)}) async-start(bf16[8,128,512]{2,1,0:T(8,128)(2,1)} %select_select_fusion), calls=%async_computation | async-start | bytes 2097152 | tf_op jit(solution)/shard_map/all_to_all | solution.py:39
  31.9 102.4 %all-gather.2.cloned.1.call-start = ((), (), s32[]{:S(2)}) async-start(), calls=%async_computation.3 | async-start | bytes 8912896 | tf_op jit(solution)/shard_map/all_gather | solution.py:47
  49.5 13.5 %collective-permute-start = (bf16[64,4096]{1,0:T(8,128)(2,1)S(1)}, bf16[64,4096]{1,0:T(8,128)(2,1)S(1)}, u32[]{:S(2)}, u32[]{:S(2)}) collective-permute-start(bf16[64,4096]{1,0:T(8,128)(2,1)S(1)} %copy.29), channel_id=1, source_target_pairs={{0,8},{8,0},{16,24},{24,16},{32,40},{40,32},{48,56},{56,48},{64,72... | collective-permute-start | bytes 1572872 | tf_op jit(solution)/shard_map/ppermute | solution.py:10
  64.0 196.7 %reduce-scatter.2.cloned.1.call-start = ((), (), s32[]{:S(2)}) async-start(), calls=%async_computation.4 | async-start | bytes 8912896 | tf_op jit(solution)/shard_map/reduce_scatter | solution.py:54
  134.3 12.5 %copy-start.1 = (bf16[1024,4096]{1,0:T(8,128)(2,1)S(1)}, bf16[1024,4096]{1,0:T(8,128)(2,1)}, u32[]{:S(2)}) copy-start(bf16[1024,4096]{1,0:T(8,128)(2,1)} %all-gather.2.cloned.1.call-done) | copy-start | bytes 25165828
  307.8 13.4 %collective-permute-start.1 = (bf16[64,8,512]{2,1,0:T(8,128)(2,1)S(1)}, bf16[64,8,512]{2,1,0:T(8,128)(2,1)S(1)}, u32[]{:S(2)}, u32[]{:S(2)}) collective-permute-start(bf16[64,8,512]{2,1,0:T(8,128)(2,1)S(1)} %bitcast.34), channel_id=1, source_target_pairs={{0,8},{8,0},{16,24},{24,16},{32,40},{40,32},{48,56},{56,48},{64,72... | collective-permute-start | bytes 1572872 | tf_op jit(solution)/shard_map/ppermute | solution.py:10
Sparse Core Ops, SparseCore 0:
  64.1 70.0 all-gather.1
  176.1 84.5 reduce-scatter.1
where the time goes:
time: 330 us; the launch traced here: 329 us
  waiting for transfers between devices  194 us (59%)
  matrix products  42.1 us (13%)
  blocking collectives  30.6 us (9%)
  other arithmetic  28.8 us (9%)
  between operations  13.6 us (4%)
  local copies, waits for them, and re-layouts  13.3 us (4%)
  starting transfers between devices  6.86 us (2%)
    reduce_scatter x1, waiting for transfers between devices, on_device(): lax.psum_scatter(lax.optimization_barrier(partial_value).astype(jnp.float...  84.8 us
    all_gather x1, waiting for transfers between devices, on_device(): rows_piece = lax.all_gather(merged, 'dp', axis=0, tiled=True)  70 us
    ppermute x2, waiting for transfers between devices, from_partner(): lax.ppermute(value, axis, [(i, i ^ 1 << stride) for i in range(lax.axis_s...  23.3 us
    unnamed x1, other arithmetic  22.6 us
    psum x1, blocking collectives, on_device(): square_sums = lax.psum(jnp.sum(tokens_f32 * tokens_f32, axis=1), 'expert')  16 us
    all_to_all x1, waiting for transfers between devices, on_device(): lax.all_to_all(chosen, 'expert', split_axis=0, concat_axis=2, tiled=True)[0]  15.8 us
    dot_general x1, matrix products, on_device(): jnp.dot(rows_piece, gate_weights, preferred_element_type=jnp.float32)  15.1 us
    all_to_all x1, blocking collectives, on_device(): lax.all_to_all(summed[:, None, :], 'expert', split_axis=2, concat_axis=1,...  14.6 us
  transfers between devices with their start and end apart: 5, of which 5 were waited for; matrix products, arithmetic and copies ran while one was open for 0% of the time, Pallas kernels for 0%

commit v1 on v0

--- a/solution.py
+++ b/solution.py
@@ -57,7 +57,20 @@
         scatter_dimension=0,
         tiled=True,
     )
-    spread = lax.all_to_all(summed[:, None, :], "expert", split_axis=2, concat_axis=1, tiled=True)
+    x = summed[:, None, :]
+    ways, here = (lax.axis_size("expert"), lax.axis_index("expert"))
+    width = x.shape[2] // ways
+    dims = list(x.shape)
+    dims[2] = width
+    height = dims[1]
+    dims[1] = height * ways
+    full = jnp.zeros(dims, x.dtype)
+    for mask in range(ways):
+        part = lax.dynamic_slice_in_dim(x, (here ^ mask) * width, width, axis=2)
+        if mask:
+            part = lax.ppermute(part, "expert", [(d, d ^ mask) for d in range(ways)])
+        full = lax.dynamic_update_slice_in_dim(full, part, (here ^ mask) * height, axis=1)
+    spread = full
     other_half = from_partner(spread, "dp", 0)
     assembled = jnp.where(
         half_bit == 0,

time: 330 us -> 301 us (0.912)
  other arithmetic: 28.8 us -> 6.14 us
  blocking collectives: 30.6 us -> 16 us
  starting transfers between devices: 6.86 us -> 15.1 us
    unnamed x1, other arithmetic: 22.6 us -> 0.01 us
    all_to_all x1 -> x0, blocking collectives: 14.6 us -> none  [on_device(): lax.all_to_all(summed[:, None, :], 'expert', split_axis=2, concat_axis=1,...]
    dynamic_update_slice x0 -> x8, local copies, waits for them, and re-layouts: none -> 9.33 us  [on_device(): lax.dynamic_update_slice_in_dim(full, part, (here ^ mask) * height, axis=1)]
    ppermute x0 -> x7, starting transfers between devices: none -> 8.22 us  [on_device(): part = lax.ppermute(part, 'expert', [(d, d ^ mask) for d in range(ways)])]
    broadcast_in_dim x1, local copies, waits for them, and re-layouts: 4.86 us -> 0.04 us  [on_device(): full = jnp.zeros(dims, x.dtype)]
  transfers between devices with their start and end apart: 5 -> 12, of which waited for: 5 -> 5; matrix products, arithmetic and copies ran while one was open for 0% -> 3% of each run, Pallas kernels for 0% -> 0%
where the time goes in v1:
time: 301 us; the launch traced here: 300 us
  waiting for transfers between devices  195 us (65%)
  matrix products  39.4 us (13%)
  blocking collectives  16 us (5%)
  starting transfers between devices  15.1 us (5%)
  local copies, waits for them, and re-layouts  14.9 us (5%)
  between operations  13.8 us (5%)
  other arithmetic  6.14 us (2%)
    reduce_scatter x1, waiting for transfers between devices, on_device(): lax.psum_scatter(lax.optimization_barrier(partial_value).astype(jnp.float...  84.7 us
    all_gather x1, waiting for transfers between devices, on_device(): rows_piece = lax.all_gather(merged, 'dp', axis=0, tiled=True)  70 us
    ppermute x2, waiting for transfers between devices, from_partner(): lax.ppermute(value, axis, [(i, i ^ 1 << stride) for i in range(lax.axis_s...  24.1 us
    psum x1, blocking collectives, on_device(): square_sums = lax.psum(jnp.sum(tokens_f32 * tokens_f32, axis=1), 'expert')  16 us
    all_to_all x1, waiting for transfers between devices, on_device(): lax.all_to_all(chosen, 'expert', split_axis=0, concat_axis=2, tiled=True)[0]  15.8 us
    dot_general x1, matrix products, on_device(): jnp.dot(rows_piece, gate_weights, preferred_element_type=jnp.float32)  15.2 us
    dot_general x1, matrix products, on_device(): jnp.dot(rows_piece, up_weights, preferred_element_type=jnp.float32)  12.5 us
    dot_general x1, matrix products, on_device(): jnp.dot(hidden, down_weights, preferred_element_type=jnp.float32)  11.3 us
  transfers between devices with their start and end apart: 12, of which 5 were waited for; matrix products, arithmetic and copies ran while one was open for 3% of the time, Pallas kernels for 0%

profile of v1, /device:TPU:0, one launch (start us, length us, event | category | flops | bytes accessed | tf_op | source)
XLA Modules:
  0.0 300.0 jit_solution(6768124152524399149)
XLA Ops:
  6.5 0.9 dynamic-slice_reduce_fusion.1
  7.5 1.1 fusion.12
  8.6 16.0 %psum.7 = f32[256]{0:T(256)S(1)} all-reduce(f32[256]{0:T(256)S(1)} %fusion.12), channel_id=1, replica_groups=mesh['dp'=16,'expert'=8] {'expert'}, use_global_device_ids=true, to_apply=%region_1.2 | all-reduce | flops 256 | bytes 2048 | tf_op jit(solution)/shard_map/psum | solution.py:29
  24.5 1.1 fusion.13
  25.6 0.9 fusion.15
  26.5 0.6 gather_fusion
  27.2 1.2 select_select_fusion
  28.3 3.6 %all-to-all-start = ((bf16[8,128,512]{2,1,0:T(8,128)(2,1)}), bf16[8,128,512]{2,1,0:T(8,128)(2,1)S(1)}, u32[]{:S(2)}, u32[]{:S(2)}) async-start(bf16[8,128,512]{2,1,0:T(8,128)(2,1)} %select_select_fusion), calls=%async_computation | async-start | bytes 2097152 | tf_op jit(solution)/shard_map/all_to_all | solution.py:39
  32.0 15.8 %all-to-all-done = bf16[8,128,512]{2,1,0:T(8,128)(2,1)S(1)} async-done(((bf16[8,128,512]{2,1,0:T(8,128)(2,1)}), bf16[8,128,512]{2,1,0:T(8,128)(2,1)S(1)}, u32[]{:S(2)}, u32[]{:S(2)}) %all-to-all-start) | async-done | bytes 1048608 | tf_op jit(solution)/shard_map/all_to_all | solution.py:39
  47.8 0.7 copy.40
  48.5 0.6 constant_dynamic-slice_fusion
  49.1 0.4 copy.42
  49.5 1.6 collective-permute-start
  51.0 0.4 copy.52
  51.4 11.6 %collective-permute-done = bf16[64,4096]{1,0:T(8,128)(2,1)S(1)} collective-permute-done((bf16[64,4096]{1,0:T(8,128)(2,1)S(1)}, bf16[64,4096]{1,0:T(8,128)(2,1)S(1)}, u32[]{:S(2)}, u32[]{:S(2)}) %collective-permute-start) | collective-permute-done | bytes 524320 | tf_op jit(solution)/shard_map/ppermute | solution.py:10
  63.0 1.0 add.121
  64.0 0.2 reduce-scatter.2.cloned.1.call-start
  64.2 70.0 %all-gather.2.cloned.1.call-done = bf16[1024,4096]{1,0:T(8,128)(2,1)} async-done(((bf16[64,4096]{1,0:T(8,128)(2,1)}), bf16[1024,4096]{1,0:T(8,128)(2,1)}) %all-gather.2.cloned.1.call-update) | async-done | bytes 8388624 | tf_op jit(solution)/shard_map/all_gather | solution.py:47
  134.3 12.5 %fusion.1 = f32[1024,896]{1,0:T(8,128)S(1)} fusion(bf16[1024,4096]{1,0:T(8,128)(2,1)} %all-gather.2.cloned.1.call-done, bf16[1,4096,896]{2,1,0:T(8,128)(2,1)} %param.9), kind=kOutput, calls=%fused_computation.3 | convolution fusion | flops 7516192768 | bytes 19398656 | tf_op jit(solution)/shard_map/dot_general | solution.py:49
  146.8 15.2 %fusion.3 = f32[1024,896]{1,0:T(8,128)S(1)} fusion(bf16[1024,4096]{1,0:T(8,128)(2,1)S(1)} %copy-done.1, bf16[1,4096,896]{2,1,0:T(8,128)(2,1)} %param.8), kind=kOutput, calls=%fused_computation.5 | convolution fusion | flops 7516192768 | bytes 19398656 | tf_op jit(solution)/shard_map/dot_general | solution.py:48
  162.0 11.3 %convolution_convert_fusion = bf16[1024,4096]{1,0:T(8,128)(2,1)} fusion(bf16[1,896,4096]{2,1,0:T(8,128)(2,1)S(1)} %bitcast.40, f32[1024,896]{1,0:T(8,128)S(1)} %fusion.1, f32[1024,896]{1,0:T(8,128)S(1)} %fusion.3), kind=kOutput, calls=%fused_computation.1 | convolution fusion | flops 7525892096 | bytes 23068672 | tf_op jit(solution)/shard_map/dot_general | solution.py:51
  173.4 84.7 %reduce-scatter.2.cloned.1.call-done = bf16[64,4096]{1,0:T(8,128)(2,1)} async-done(((bf16[1024,4096]{1,0:T(8,128)(2,1)}), bf16[64,4096]{1,0:T(8,128)(2,1)}) %reduce-scatter.2.cloned.1.call-update) | async-done | bytes 524304 | tf_op jit(solution)/shard_map/reduce_scatter | solution.py:54
  258.1 1.1 dynamic-slice_bitcast_fusion
  259.3 1.7 collective-permute-start.2
  260.9 0.2 collective-permute-start.3
  261.1 3.2 %collective-permute-start.4 = (bf16[64,1,512]{2,0,1:T(8,128)(2,1)S(1)}, bf16[64,1,512]{2,0,1:T(8,128)(2,1)S(1)}, u32[]{:S(2)}, u32[]{:S(2)}) collective-permute-start(bf16[64,1,512]{2,0,1:T(8,128)(2,1)S(1)} %get-tuple-element.12), channel_id=1, source_target_pairs={{0,4},{1,5},{2,6},{3,7},{4,0},{5,1},{6,2},{7,3},{8,12},{9,13},{10,... | collective-permute-start | bytes 196616 | tf_op jit(solution)/shard_map/ppermute | solution.py:71
  264.4 2.9 collective-permute-start.6
  267.3 0.1 collective-permute-start.7
  267.6 1.2 dynamic_update_slice.24
  268.7 0.1 copy.44
  268.9 1.2 dynamic_update_slice.25
  270.0 0.1 copy.45
  270.1 1.2 dynamic_update_slice.26
  271.3 0.1 copy.46
  271.4 1.2 dynamic_update_slice.27
  272.6 0.1 copy.47
  272.7 1.2 dynamic_update_slice.28
  273.9 0.1 copy.48
  274.0 1.2 dynamic_update_slice.29
  275.2 0.1 copy.49
  275.3 1.2 dynamic_update_slice.30
  276.5 0.1 copy.50
  276.6 1.2 dynamic_update_slice.31
  277.8 1.5 collective-permute-start.8
  279.3 0.2 dynamic-slice_reduce_fusion
  279.5 12.5 %collective-permute-done.8 = bf16[64,8,512]{2,1,0:T(8,128)(2,1)S(1)} collective-permute-done((bf16[64,8,512]{2,1,0:T(8,128)(2,1)S(1)}, bf16[64,8,512]{2,1,0:T(8,128)(2,1)S(1)}, u32[]{:S(2)}, u32[]{:S(2)}) %collective-permute-start.8) | collective-permute-done | bytes 524320 | tf_op jit(solution)/shard_map/ppermute | solution.py:10
  292.0 0.4 convolution_convert_fusion.1
  292.4 0.7 copy.51
  (27 shorter events, 0.4 us)
Async XLA Ops:
  6.5 272.8 %copy-start = (f32[8,8]{1,0:T(8,128)S(1)}, f32[8,8]{1,0:T(8,128)}, u32[]{:S(2)}) copy-start(f32[8,8]{1,0:T(8,128)} %param.13) | copy-start | bytes 772
  28.3 19.4 %all-to-all-start = ((bf16[8,128,512]{2,1,0:T(8,128)(2,1)}), bf16[8,128,512]{2,1,0:T(8,128)(2,1)S(1)}, u32[]{:S(2)}, u32[]{:S(2)}) async-start(bf16[8,128,512]{2,1,0:T(8,128)(2,1)} %select_select_fusion), calls=%async_computation | async-start | bytes 2097152 | tf_op jit(solution)/shard_map/all_to_all | solution.py:39
  31.9 102.3 %all-gather.2.cloned.1.call-start = ((), (), s32[]{:S(2)}) async-start(), calls=%async_computation.2 | async-start | bytes 8912896 | tf_op jit(solution)/shard_map/all_gather | solution.py:47
  49.5 13.5 %collective-permute-start = (bf16[64,4096]{1,0:T(8,128)(2,1)S(1)}, bf16[64,4096]{1,0:T(8,128)(2,1)S(1)}, u32[]{:S(2)}, u32[]{:S(2)}) collective-permute-start(bf16[64,4096]{1,0:T(8,128)(2,1)S(1)} %copy.42), channel_id=1, source_target_pairs={{0,8},{8,0},{16,24},{24,16},{32,40},{40,32},{48,56},{56,48},{64,72... | collective-permute-start | bytes 1572872 | tf_op jit(solution)/shard_map/ppermute | solution.py:10
  64.0 194.1 %reduce-scatter.2.cloned.1.call-start = ((), (), s32[]{:S(2)}) async-start(), calls=%async_computation.3 | async-start | bytes 8912896 | tf_op jit(solution)/shard_map/reduce_scatter | solution.py:54
  134.2 12.5 %copy-start.1 = (bf16[1024,4096]{1,0:T(8,128)(2,1)S(1)}, bf16[1024,4096]{1,0:T(8,128)(2,1)}, u32[]{:S(2)}) copy-start(bf16[1024,4096]{1,0:T(8,128)(2,1)} %all-gather.2.cloned.1.call-done) | copy-start | bytes 25165828
  134.3 27.7 %slice-start = ((s8[7340032]{0:T(1024)(128)(4,1)}), s8[4194304]{0:T(1024)(128)(4,1)S(1)}, s32[]{:S(2)}) async-start(s8[7340032]{0:T(1024)(128)(4,1)} %bitcast.39), calls=%async_computation.4 | async-start | bytes 8388608
  146.8 15.2 %slice-start.1 = ((s8[7340032]{0:T(1024)(128)(4,1)}), s8[3145728]{0:T(1024)(128)(4,1)S(1)}, s32[]{:S(2)}) async-start(s8[7340032]{0:T(1024)(128)(4,1)} %bitcast.39), calls=%async_computation.5 | async-start | bytes 6291456
  259.2 5.2 %collective-permute-start.1 = (bf16[64,1,512]{2,0,1:T(8,128)(2,1)S(1)}, bf16[64,1,512]{2,0,1:T(8,128)(2,1)S(1)}, u32[]{:S(2)}, u32[]{:S(2)}) collective-permute-start(bf16[64,1,512]{2,0,1:T(8,128)(2,1)S(1)} %get-tuple-element.15), channel_id=1, source_target_pairs={{0,1},{1,0},{2,3},{3,2},{4,5},{5,4},{6,7},{7,6},{8,9},{9,8},{10,11... | collective-permute-start | bytes 196616 | tf_op jit(solution)/shard_map/ppermute | solution.py:71
  259.3 8.0 %collective-permute-start.2 = (bf16[64,1,512]{2,0,1:T(8,128)(2,1)S(1)}, bf16[64,1,512]{2,0,1:T(8,128)(2,1)S(1)}, u32[]{:S(2)}, u32[]{:S(2)}) collective-permute-start(bf16[64,1,512]{2,0,1:T(8,128)(2,1)S(1)} %get-tuple-element.14), channel_id=1, source_target_pairs={{0,2},{1,3},{2,0},{3,1},{4,6},{5,7},{6,4},{7,5},{8,10},{9,11},{10,... | collective-permute-start | bytes 196616 | tf_op jit(solution)/shard_map/ppermute | solution.py:71
  260.9 10.4 %collective-permute-start.3 = (bf16[64,1,512]{2,0,1:T(8,128)(2,1)S(1)}, bf16[64,1,512]{2,0,1:T(8,128)(2,1)S(1)}, u32[]{:S(2)}, u32[]{:S(2)}) collective-permute-start(bf16[64,1,512]{2,0,1:T(8,128)(2,1)S(1)} %get-tuple-element.13), channel_id=1, source_target_pairs={{0,3},{1,2},{2,1},{3,0},{4,7},{5,6},{6,5},{7,4},{8,11},{9,10},{10,... | collective-permute-start | bytes 196616 | tf_op jit(solution)/shard_map/ppermute | solution.py:71
  261.1 11.5 %collective-permute-start.4 = (bf16[64,1,512]{2,0,1:T(8,128)(2,1)S(1)}, bf16[64,1,512]{2,0,1:T(8,128)(2,1)S(1)}, u32[]{:S(2)}, u32[]{:S(2)}) collective-permute-start(bf16[64,1,512]{2,0,1:T(8,128)(2,1)S(1)} %get-tuple-element.12), channel_id=1, source_target_pairs={{0,4},{1,5},{2,6},{3,7},{4,0},{5,1},{6,2},{7,3},{8,12},{9,13},{10,... | collective-permute-start | bytes 196616 | tf_op jit(solution)/shard_map/ppermute | solution.py:71
  264.3 9.6 %collective-permute-start.5 = (bf16[64,1,512]{2,0,1:T(8,128)(2,1)S(1)}, bf16[64,1,512]{2,0,1:T(8,128)(2,1)S(1)}, u32[]{:S(2)}, u32[]{:S(2)}) collective-permute-start(bf16[64,1,512]{2,0,1:T(8,128)(2,1)S(1)} %get-tuple-element.11), channel_id=1, source_target_pairs={{0,5},{1,4},{2,7},{3,6},{4,1},{5,0},{6,3},{7,2},{8,13},{9,12},{10,... | collective-permute-start | bytes 196616 | tf_op jit(solution)/shard_map/ppermute | solution.py:71
  264.4 10.8 %collective-permute-start.6 = (bf16[64,1,512]{2,0,1:T(8,128)(2,1)S(1)}, bf16[64,1,512]{2,0,1:T(8,128)(2,1)S(1)}, u32[]{:S(2)}, u32[]{:S(2)}) collective-permute-start(bf16[64,1,512]{2,0,1:T(8,128)(2,1)S(1)} %get-tuple-element.10), channel_id=1, source_target_pairs={{0,6},{1,7},{2,4},{3,5},{4,2},{5,3},{6,0},{7,1},{8,14},{9,15},{10,... | collective-permute-start | bytes 196616 | tf_op jit(solution)/shard_map/ppermute | solution.py:71
  267.3 9.2 %collective-permute-start.7 = (bf16[64,1,512]{2,0,1:T(8,128)(2,1)S(1)}, bf16[64,1,512]{2,0,1:T(8,128)(2,1)S(1)}, u32[]{:S(2)}, u32[]{:S(2)}) collective-permute-start(bf16[64,1,512]{2,0,1:T(8,128)(2,1)S(1)} %get-tuple-element.9), channel_id=1, source_target_pairs={{0,7},{1,6},{2,5},{3,4},{4,3},{5,2},{6,1},{7,0},{8,15},{9,14},{10,... | collective-permute-start | bytes 196616 | tf_op jit(solution)/shard_map/ppermute | solution.py:71
  277.8 14.2 %collective-permute-start.8 = (bf16[64,8,512]{2,1,0:T(8,128)(2,1)S(1)}, bf16[64,8,512]{2,1,0:T(8,128)(2,1)S(1)}, u32[]{:S(2)}, u32[]{:S(2)}) collective-permute-start(bf16[64,8,512]{2,1,0:T(8,128)(2,1)S(1)} %dynamic_update_slice.31), channel_id=1, source_target_pairs={{0,8},{8,0},{16,24},{24,16},{32,40},{40,32},{48,56},{56,48},{64,72... | collective-permute-start | bytes 1572872 | tf_op jit(solution)/shard_map/ppermute | solution.py:10
Sparse Core Ops, SparseCore 0:
  64.1 70.0 all-gather.1
  173.5 84.5 reduce-scatter.1
